TPU v7x, 128 devices: a whole 4x4x4 slice. The times are simulated.
128 devices in a mesh: seq: 16 (over z, x), ctx: 8 (over y, core).
Axes of the slice: x: 4, y: 4, z: 4, core: 2. Of those that a mesh axis runs over, the one named last changes fastest.
Arguments:
- queries: bfloat16 [8192, 4096], P(('seq', 'ctx')), may hold values from -90 to 90
- stretch_kv: bfloat16 [2, 8192, 1024], P(None, ('seq', 'ctx')), may hold values from -4.1 to 4.1
- cache_kv: bfloat16 [1024, 2, 8, 128, 128], P('ctx', None, None, 'seq'), may hold values from -4 to 4
- vertical: int32 [32, 8], replicated, may hold values from 0 to 1023, as said below
- slash: int32 [32, 24], replicated, may hold values from 0 to 1023
- owner_map: int32 [1024], replicated, may hold values from 0 to 1023, as said below
Outputs:
- attended: bfloat16 [8192, 4096], P(('seq', 'ctx'))
Inputs may be any that keep to these rules, and one draw needn't show every extreme that they name: For every head the 8 vertical blocks and the blocks 1024 - 1 - s of its slash entries s are 32 distinct blocks; for every head exactly 12 of them have storage rows in one range g * 128 to (g + 1) * 128 - 1, and at most 3 in each other such range, with exactly 3 in some. `owner_map`: each storage row appears once.
All inputs are finite; a program needn't handle non-finite values.
Results may differ from a plain program's by a relative error of at most 0.0075.
Values may be sent and summed in bfloat16 or wider, within the bound.
A program may use at most 128 MiB of HBM per device.

v0:
```python
import jax
import jax.numpy as jnp
from jax import lax
from jax.sharding import PartitionSpec as P

H = 32
KVH = 8
HD = 128
BLK = 128
CAP = 12
masked_value = -1e30


def stretch_positions(rows, shard, tok_rows, n_ctx):
    return (rows // tok_rows * n_ctx + shard) * tok_rows + rows % tok_rows


def online_update(carry, scores, visible, mixing):
    running_max, running_sum, weighted = carry
    masked = jnp.where(visible, scores, masked_value)
    new_max = jnp.maximum(running_max, jnp.max(masked, axis=2, keepdims=True))
    weights = jnp.where(visible, jnp.exp(masked - new_max), 0.0)
    fading = jnp.exp(running_max - new_max)
    new_sum = running_sum * fading + jnp.sum(weights, axis=2, keepdims=True)
    new_weighted = weighted * fading + mixing(weights.astype(jnp.bfloat16))
    return (new_max, new_sum, new_weighted)


def owner_slots(owner, local_row, owner_group):
    owned = owner == owner_group
    slot_rank = jnp.cumsum(owned.astype(jnp.int32), axis=1) - 1
    slot_hit = owned[:, :, None] & (
        slot_rank[:, :, None] == jnp.arange(CAP, dtype=jnp.int32)[None, None, :]
    )
    slot_row = jnp.sum(jnp.where(slot_hit, local_row[:, :, None], 0), axis=1)
    return (slot_row, jnp.any(slot_hit, axis=1))


def on_device(queries, stretch_kv, cache_kv, vertical, slash, owner_map):
    n_seq = lax.axis_size("seq")
    n_ctx = lax.axis_size("ctx")
    seq_index = lax.axis_index("seq")
    ctx_index = lax.axis_index("ctx")
    tok_rows = queries.shape[0]
    per_device = H // n_seq
    query_rows = tok_rows * n_seq
    score_scale = HD ** (-0.5)
    sent_queries = queries.reshape(tok_rows, n_seq, per_device * HD)
    own_queries = lax.all_to_all(
        sent_queries, "seq", split_axis=1, concat_axis=0, tiled=True
    ).reshape(query_rows, per_device, HD)
    widened_kv = jnp.repeat(stretch_kv.reshape(2, tok_rows, KVH, HD), n_seq // KVH, axis=2)
    own_kv = lax.all_to_all(widened_kv, "seq", split_axis=2, concat_axis=1, tiled=True).reshape(
        2, query_rows, HD
    )
    row_index = jnp.arange(query_rows, dtype=jnp.int32)
    query_position = stretch_positions(row_index, ctx_index, tok_rows, n_ctx)
    start_carry = (
        jnp.full((per_device, query_rows, 1), masked_value, jnp.float32),
        jnp.zeros((per_device, query_rows, 1), jnp.float32),
        jnp.zeros((per_device, query_rows, HD), jnp.float32),
    )
    piece = lax.all_gather(own_kv, "ctx", axis=1, tiled=True)

    def visit(index, inner):
        shard_kv = lax.dynamic_slice_in_dim(piece, index * query_rows, query_rows, 1)
        key_position = stretch_positions(row_index, index, tok_rows, n_ctx)
        scores = (
            jnp.einsum("qpd,kd->pqk", own_queries, shard_kv[0], preferred_element_type=jnp.float32)
            * score_scale
        )
        visible = (key_position[None, :] <= query_position[:, None])[None]

        def stretch_mix(rounded):
            return jnp.einsum(
                "pqk,kd->pqd", rounded, shard_kv[1], preferred_element_type=jnp.float32
            )

        return online_update(inner, scores, visible, stretch_mix)

    carry = lax.fori_loop(0, piece.shape[1] // query_rows, visit, start_carry)
    blk_ctx = cache_kv.shape[0]
    part_rows = cache_kv.shape[3]
    total_blocks = blk_ctx * n_ctx
    selected = jnp.concatenate([vertical, total_blocks - 1 - slash], axis=1)
    storage = owner_map[selected]
    owner = storage // blk_ctx
    local_row = storage % blk_ctx
    send_rows, send_hit = owner_slots(owner, local_row, ctx_index)
    head_kv = jnp.arange(H, dtype=jnp.int32) // (H // KVH)

    def group_valid(owner_group):
        return owner_slots(owner, local_row, owner_group)[1]

    valid_all = jax.vmap(group_valid)(jnp.arange(n_ctx, dtype=jnp.int32))
    own_valid = lax.dynamic_slice_in_dim(valid_all, seq_index * per_device, per_device, 1)
    packed = cache_kv[send_rows, :, head_kv[:, None]]
    packed = packed.reshape(n_seq, per_device, CAP, 2, part_rows, HD)
    widened = jnp.broadcast_to(packed[:, None], (n_seq, n_ctx) + packed.shape[1:]).reshape(
        (n_seq * n_ctx, 1) + packed.shape[1:]
    )
    received = lax.all_to_all(widened, ("seq", "ctx"), split_axis=0, concat_axis=1, tiled=True)
    arranged = received.reshape((n_seq, n_ctx) + packed.shape[1:])
    arranged = jnp.transpose(arranged, (2, 1, 3, 4, 0, 5, 6)).reshape(
        per_device, n_ctx * CAP, 2, BLK, HD
    )
    fold_piece = arranged

    def visit(index, inner):
        blocks = lax.dynamic_slice_in_dim(fold_piece, index * CAP, CAP, 1)
        owner_group = 0 // CAP + index
        live_slots = lax.dynamic_index_in_dim(own_valid, owner_group, 0, keepdims=False)
        block_keys = blocks[:, :, 0].reshape(per_device, CAP * BLK, HD)
        block_values = blocks[:, :, 1].reshape(per_device, CAP * BLK, HD)
        scores = (
            jnp.einsum("qpd,pkd->pqk", own_queries, block_keys, preferred_element_type=jnp.float32)
            * score_scale
        )
        visible = jnp.repeat(live_slots, BLK, axis=1)[:, None, :]

        def block_mix(rounded):
            return jnp.einsum(
                "pqk,pkd->pqd", rounded, block_values, preferred_element_type=jnp.float32
            )

        return online_update(inner, scores, visible, block_mix)

    carry = lax.fori_loop(0, fold_piece.shape[1] // CAP, visit, carry)
    running_max, running_sum, weighted = carry
    attended = (weighted / running_sum).astype(jnp.bfloat16)
    outgoing = jnp.transpose(attended, (1, 0, 2)).reshape(n_seq, tok_rows, per_device * HD)
    returned = lax.all_to_all(outgoing, "seq", split_axis=0, concat_axis=2, tiled=True)
    return returned.reshape(tok_rows, H * HD)


def solution(mesh):
    placed = (
        P(("seq", "ctx"), None),
        P(None, ("seq", "ctx"), None),
        P("ctx", None, None, "seq", None),
        P(),
        P(),
        P(),
    )
    return jax.shard_map(
        on_device, mesh=mesh, in_specs=placed, out_specs=P(("seq", "ctx"), None), check_vma=False
    )
```

profile of v0, /device:TPU:9, one launch (start us, length us, event | category | flops | bytes accessed | tf_op | source)
XLA Modules:
  0.0 366.4 jit_solution(12740948286434524157)
XLA Ops:
  7.7 17.9 %all_to_all.54 = bf16[2,64,16,128]{3,1,0,2:T(8,128)(2,1)S(1)} all-to-all(bf16[2,64,16,128]{3,1,0,2:T(8,128)(2,1)S(1)} %bitcast.179), channel_id=1, replica_groups=mesh['seq'=16,'ctx'=8] {'seq'}, dimensions={2} | all-to-all | bytes 1048576 | tf_op jit(solution)/shard_map/all_to_all | solution.py:53
  26.4 1.9 copy.84
  28.3 3.6 all-to-all-start.1
  33.5 4.5 %gather_fusion = s32[1024]{0:T(1024)S(1)} fusion(s32[1024]{0:T(1024)S(1)} %copy-done.2, s32[1024]{0:T(1024)S(1)} %broadcast_clamp_fusion), kind=kCustom, calls=%fused_computation | custom fusion | bytes 12288 | tf_op jit(solution)/shard_map/gather | solution.py:86
  38.1 1.5 reduce_window_sum.22
  39.9 1.7 fusion.57
  42.4 5.2 %gather_fusion.1 = bf16[384,2,8,128]{3,2,1,0:T(8,128)(2,1)S(1)} fusion(bf16[128,2,8,8,128]{4,3,2,1,0:T(8,128)(2,1)} %param.12, s32[384]{0:T(512)S(1)} %reshape.354), kind=kCustom, calls=%fused_computation.1 | custom fusion | bytes 3148800 | tf_op jit(solution)/shard_map/gather | solution.py:97
  47.6 8.0 %broadcast_in_dim.202 = bf16[16,8,2,12,2,8,128]{6,5,4,3,2,1,0:T(8,128)(2,1)} broadcast(bf16[16,2,12,2,8,128]{5,4,3,2,1,0:T(8,128)(2,1)S(1)} %bitcast.169), dimensions={0,2,3,4,5,6} | broadcast | bytes 14155776 | tf_op jit(solution)/shard_map/broadcast_in_dim | solution.py:99
  55.6 11.8 %all-to-all-start.2 = ((bf16[128,1,2,12,2,8,128]{6,5,4,3,2,1,0:T(8,128)(2,1)}), bf16[128,1,2,12,2,8,128]{6,5,4,3,2,1,0:T(8,128)(2,1)}, u32[]{:S(2)}, u32[]{:S(2)}) async-start(bf16[128,1,2,12,2,8,128]{6,5,4,3,2,1,0:T(8,128)(2,1)} %bitcast.166), calls=%async_computation.2 | async-start | bytes 25165824 | tf_op jit(solution)/shard_map/all_to_all | solution.py:102
  67.6 133.7 %while.41 = (s32[]{:T(128)}, f32[2,1024,1]{1,0,2:T(2,128)S(1)}, f32[2,1024,1]{1,0,2:T(2,128)S(1)}, f32[2,1024,128]{2,1,0:T(8,128)S(1)}, bf16[2,8192,128]{2,1,0:T...) while((s32[]{:T(128)}, f32[2,1024,1]{1,0,2:T(2,128)S(1)}, ...), condition=%wide.region_3.4_spmd.clone.clone, body=%wide.region_0.3_spmd.clone.clone.sunk | while | flops 1102876672 | bytes 32655572 | solution.py:81
  68.3 6.0 %fusion.98 = (f32[2,1024]{1,0:T(2,128)S(1)}, f32[1024,1024,2]{1,0,2:T(8,128)}) fusion(pred[1024,1024]{0,1:T(8,128)(4,1)S(1)} %broadcast_compare_fusion.4, bf16[1024,2,128]{2,0,1:T(8,128)(2,1)S(1)} %get-tuple-element.746, bf16[2,8192,128]{2,1,0:T(8,128)(2,1)} %get-tuple-element.745, s32[]{:T(128)S(6)} %select_n.332), kind=kOutput, calls=%fused_computation.32.clone.1 | convolution fusion | flops 543160320 | bytes 10231812 | tf_op jit(solution)/shard_map/while/body/eval_jaxpr/qpd,kd->pqk/dot_general | solution.py:69
  74.3 4.6 %fusion.100 = f32[2,1024]{1,0:T(2,128)S(1)} fusion(f32[1024,1024,2]{1,0,2:T(8,128)} %get-tuple-element.715, f32[2,1024]{1,0:T(2,128)S(1)} %bitcast.175, pred[1024,1024]{0,1:T(8,128)(4,1)S(1)} %broadcast_compare_fusion.4), kind=kLoop, calls=%fused_computation.34.clone.1 | loop fusion | flops 10483712 | bytes 9453568 | tf_op jit(solution)/shard_map/while/body/eval_jaxpr/reduce_sum | solution.py:24
  78.9 5.3 %fusion.101 = f32[2,1024,128]{2,1,0:T(8,128)S(1)} fusion(f32[1024,1024,2]{1,0,2:T(8,128)} %get-tuple-element.715, f32[2,1024]{1,0:T(2,128)S(1)} %bitcast.176, pred[1024,1024]{0,1:T(8,128)(4,1)S(1)} %broadcast_compare_fusion.4, f32[2,1024,128]{2,1,0:T(8,128)S(1)} %get-tuple-element.732, f32[2,1024]{1,0:T(2,128)S(1)} %get-tuple-element.716, ...), kind=kOutput, calls=%fused_computation.38.clone.1 | convolution fusion | flops 548143104 | bytes 11812873 | tf_op jit(solution)/shard_map/while/body/eval_jaxpr/pqk,kd->pqd/dot_general | solution.py:75
  85.0 6.0 %fusion.98 = (f32[2,1024]{1,0:T(2,128)S(1)}, f32[1024,1024,2]{1,0,2:T(8,128)}) fusion(pred[1024,1024]{0,1:T(8,128)(4,1)S(1)} %broadcast_compare_fusion.4, bf16[1024,2,128]{2,0,1:T(8,128)(2,1)S(1)} %get-tuple-element.746, bf16[2,8192,128]{2,1,0:T(8,128)(2,1)} %get-tuple-element.745, s32[]{:T(128)S(6)} %select_n.332), kind=kOutput, calls=%fused_computation.32.clone.1 | convolution fusion | flops 543160320 | bytes 10231812 | tf_op jit(solution)/shard_map/while/body/eval_jaxpr/qpd,kd->pqk/dot_general | solution.py:69
  91.0 4.6 %fusion.100 = f32[2,1024]{1,0:T(2,128)S(1)} fusion(f32[1024,1024,2]{1,0,2:T(8,128)} %get-tuple-element.715, f32[2,1024]{1,0:T(2,128)S(1)} %bitcast.175, pred[1024,1024]{0,1:T(8,128)(4,1)S(1)} %broadcast_compare_fusion.4), kind=kLoop, calls=%fused_computation.34.clone.1 | loop fusion | flops 10483712 | bytes 9453568 | tf_op jit(solution)/shard_map/while/body/eval_jaxpr/reduce_sum | solution.py:24
  95.6 5.3 %fusion.101 = f32[2,1024,128]{2,1,0:T(8,128)S(1)} fusion(f32[1024,1024,2]{1,0,2:T(8,128)} %get-tuple-element.715, f32[2,1024]{1,0:T(2,128)S(1)} %bitcast.176, pred[1024,1024]{0,1:T(8,128)(4,1)S(1)} %broadcast_compare_fusion.4, f32[2,1024,128]{2,1,0:T(8,128)S(1)} %get-tuple-element.732, f32[2,1024]{1,0:T(2,128)S(1)} %get-tuple-element.716, ...), kind=kOutput, calls=%fused_computation.38.clone.1 | convolution fusion | flops 548143104 | bytes 11812873 | tf_op jit(solution)/shard_map/while/body/eval_jaxpr/pqk,kd->pqd/dot_general | solution.py:75
  101.7 6.0 %fusion.98 = (f32[2,1024]{1,0:T(2,128)S(1)}, f32[1024,1024,2]{1,0,2:T(8,128)}) fusion(pred[1024,1024]{0,1:T(8,128)(4,1)S(1)} %broadcast_compare_fusion.4, bf16[1024,2,128]{2,0,1:T(8,128)(2,1)S(1)} %get-tuple-element.746, bf16[2,8192,128]{2,1,0:T(8,128)(2,1)} %get-tuple-element.745, s32[]{:T(128)S(6)} %select_n.332), kind=kOutput, calls=%fused_computation.32.clone.1 | convolution fusion | flops 543160320 | bytes 10231812 | tf_op jit(solution)/shard_map/while/body/eval_jaxpr/qpd,kd->pqk/dot_general | solution.py:69
  107.7 4.6 %fusion.100 = f32[2,1024]{1,0:T(2,128)S(1)} fusion(f32[1024,1024,2]{1,0,2:T(8,128)} %get-tuple-element.715, f32[2,1024]{1,0:T(2,128)S(1)} %bitcast.175, pred[1024,1024]{0,1:T(8,128)(4,1)S(1)} %broadcast_compare_fusion.4), kind=kLoop, calls=%fused_computation.34.clone.1 | loop fusion | flops 10483712 | bytes 9453568 | tf_op jit(solution)/shard_map/while/body/eval_jaxpr/reduce_sum | solution.py:24
  112.3 5.3 %fusion.101 = f32[2,1024,128]{2,1,0:T(8,128)S(1)} fusion(f32[1024,1024,2]{1,0,2:T(8,128)} %get-tuple-element.715, f32[2,1024]{1,0:T(2,128)S(1)} %bitcast.176, pred[1024,1024]{0,1:T(8,128)(4,1)S(1)} %broadcast_compare_fusion.4, f32[2,1024,128]{2,1,0:T(8,128)S(1)} %get-tuple-element.732, f32[2,1024]{1,0:T(2,128)S(1)} %get-tuple-element.716, ...), kind=kOutput, calls=%fused_computation.38.clone.1 | convolution fusion | flops 548143104 | bytes 11812873 | tf_op jit(solution)/shard_map/while/body/eval_jaxpr/pqk,kd->pqd/dot_general | solution.py:75
  118.4 6.0 %fusion.98 = (f32[2,1024]{1,0:T(2,128)S(1)}, f32[1024,1024,2]{1,0,2:T(8,128)}) fusion(pred[1024,1024]{0,1:T(8,128)(4,1)S(1)} %broadcast_compare_fusion.4, bf16[1024,2,128]{2,0,1:T(8,128)(2,1)S(1)} %get-tuple-element.746, bf16[2,8192,128]{2,1,0:T(8,128)(2,1)} %get-tuple-element.745, s32[]{:T(128)S(6)} %select_n.332), kind=kOutput, calls=%fused_computation.32.clone.1 | convolution fusion | flops 543160320 | bytes 10231812 | tf_op jit(solution)/shard_map/while/body/eval_jaxpr/qpd,kd->pqk/dot_general | solution.py:69
  124.4 4.6 %fusion.100 = f32[2,1024]{1,0:T(2,128)S(1)} fusion(f32[1024,1024,2]{1,0,2:T(8,128)} %get-tuple-element.715, f32[2,1024]{1,0:T(2,128)S(1)} %bitcast.175, pred[1024,1024]{0,1:T(8,128)(4,1)S(1)} %broadcast_compare_fusion.4), kind=kLoop, calls=%fused_computation.34.clone.1 | loop fusion | flops 10483712 | bytes 9453568 | tf_op jit(solution)/shard_map/while/body/eval_jaxpr/reduce_sum | solution.py:24
  129.1 5.3 %fusion.101 = f32[2,1024,128]{2,1,0:T(8,128)S(1)} fusion(f32[1024,1024,2]{1,0,2:T(8,128)} %get-tuple-element.715, f32[2,1024]{1,0:T(2,128)S(1)} %bitcast.176, pred[1024,1024]{0,1:T(8,128)(4,1)S(1)} %broadcast_compare_fusion.4, f32[2,1024,128]{2,1,0:T(8,128)S(1)} %get-tuple-element.732, f32[2,1024]{1,0:T(2,128)S(1)} %get-tuple-element.716, ...), kind=kOutput, calls=%fused_computation.38.clone.1 | convolution fusion | flops 548143104 | bytes 11812873 | tf_op jit(solution)/shard_map/while/body/eval_jaxpr/pqk,kd->pqd/dot_general | solution.py:75
  135.1 6.0 %fusion.98 = (f32[2,1024]{1,0:T(2,128)S(1)}, f32[1024,1024,2]{1,0,2:T(8,128)}) fusion(pred[1024,1024]{0,1:T(8,128)(4,1)S(1)} %broadcast_compare_fusion.4, bf16[1024,2,128]{2,0,1:T(8,128)(2,1)S(1)} %get-tuple-element.746, bf16[2,8192,128]{2,1,0:T(8,128)(2,1)} %get-tuple-element.745, s32[]{:T(128)S(6)} %select_n.332), kind=kOutput, calls=%fused_computation.32.clone.1 | convolution fusion | flops 543160320 | bytes 10231812 | tf_op jit(solution)/shard_map/while/body/eval_jaxpr/qpd,kd->pqk/dot_general | solution.py:69
  141.1 4.6 %fusion.100 = f32[2,1024]{1,0:T(2,128)S(1)} fusion(f32[1024,1024,2]{1,0,2:T(8,128)} %get-tuple-element.715, f32[2,1024]{1,0:T(2,128)S(1)} %bitcast.175, pred[1024,1024]{0,1:T(8,128)(4,1)S(1)} %broadcast_compare_fusion.4), kind=kLoop, calls=%fused_computation.34.clone.1 | loop fusion | flops 10483712 | bytes 9453568 | tf_op jit(solution)/shard_map/while/body/eval_jaxpr/reduce_sum | solution.py:24
  145.8 5.3 %fusion.101 = f32[2,1024,128]{2,1,0:T(8,128)S(1)} fusion(f32[1024,1024,2]{1,0,2:T(8,128)} %get-tuple-element.715, f32[2,1024]{1,0:T(2,128)S(1)} %bitcast.176, pred[1024,1024]{0,1:T(8,128)(4,1)S(1)} %broadcast_compare_fusion.4, f32[2,1024,128]{2,1,0:T(8,128)S(1)} %get-tuple-element.732, f32[2,1024]{1,0:T(2,128)S(1)} %get-tuple-element.716, ...), kind=kOutput, calls=%fused_computation.38.clone.1 | convolution fusion | flops 548143104 | bytes 11812873 | tf_op jit(solution)/shard_map/while/body/eval_jaxpr/pqk,kd->pqd/dot_general | solution.py:75
  151.9 6.0 %fusion.98 = (f32[2,1024]{1,0:T(2,128)S(1)}, f32[1024,1024,2]{1,0,2:T(8,128)}) fusion(pred[1024,1024]{0,1:T(8,128)(4,1)S(1)} %broadcast_compare_fusion.4, bf16[1024,2,128]{2,0,1:T(8,128)(2,1)S(1)} %get-tuple-element.746, bf16[2,8192,128]{2,1,0:T(8,128)(2,1)} %get-tuple-element.745, s32[]{:T(128)S(6)} %select_n.332), kind=kOutput, calls=%fused_computation.32.clone.1 | convolution fusion | flops 543160320 | bytes 10231812 | tf_op jit(solution)/shard_map/while/body/eval_jaxpr/qpd,kd->pqk/dot_general | solution.py:69
  157.8 4.6 %fusion.100 = f32[2,1024]{1,0:T(2,128)S(1)} fusion(f32[1024,1024,2]{1,0,2:T(8,128)} %get-tuple-element.715, f32[2,1024]{1,0:T(2,128)S(1)} %bitcast.175, pred[1024,1024]{0,1:T(8,128)(4,1)S(1)} %broadcast_compare_fusion.4), kind=kLoop, calls=%fused_computation.34.clone.1 | loop fusion | flops 10483712 | bytes 9453568 | tf_op jit(solution)/shard_map/while/body/eval_jaxpr/reduce_sum | solution.py:24
  162.5 5.3 %fusion.101 = f32[2,1024,128]{2,1,0:T(8,128)S(1)} fusion(f32[1024,1024,2]{1,0,2:T(8,128)} %get-tuple-element.715, f32[2,1024]{1,0:T(2,128)S(1)} %bitcast.176, pred[1024,1024]{0,1:T(8,128)(4,1)S(1)} %broadcast_compare_fusion.4, f32[2,1024,128]{2,1,0:T(8,128)S(1)} %get-tuple-element.732, f32[2,1024]{1,0:T(2,128)S(1)} %get-tuple-element.716, ...), kind=kOutput, calls=%fused_computation.38.clone.1 | convolution fusion | flops 548143104 | bytes 11812873 | tf_op jit(solution)/shard_map/while/body/eval_jaxpr/pqk,kd->pqd/dot_general | solution.py:75
  168.6 6.0 %fusion.98 = (f32[2,1024]{1,0:T(2,128)S(1)}, f32[1024,1024,2]{1,0,2:T(8,128)}) fusion(pred[1024,1024]{0,1:T(8,128)(4,1)S(1)} %broadcast_compare_fusion.4, bf16[1024,2,128]{2,0,1:T(8,128)(2,1)S(1)} %get-tuple-element.746, bf16[2,8192,128]{2,1,0:T(8,128)(2,1)} %get-tuple-element.745, s32[]{:T(128)S(6)} %select_n.332), kind=kOutput, calls=%fused_computation.32.clone.1 | convolution fusion | flops 543160320 | bytes 10231812 | tf_op jit(solution)/shard_map/while/body/eval_jaxpr/qpd,kd->pqk/dot_general | solution.py:69
  174.6 4.6 %fusion.100 = f32[2,1024]{1,0:T(2,128)S(1)} fusion(f32[1024,1024,2]{1,0,2:T(8,128)} %get-tuple-element.715, f32[2,1024]{1,0:T(2,128)S(1)} %bitcast.175, pred[1024,1024]{0,1:T(8,128)(4,1)S(1)} %broadcast_compare_fusion.4), kind=kLoop, calls=%fused_computation.34.clone.1 | loop fusion | flops 10483712 | bytes 9453568 | tf_op jit(solution)/shard_map/while/body/eval_jaxpr/reduce_sum | solution.py:24
  179.2 5.3 %fusion.101 = f32[2,1024,128]{2,1,0:T(8,128)S(1)} fusion(f32[1024,1024,2]{1,0,2:T(8,128)} %get-tuple-element.715, f32[2,1024]{1,0:T(2,128)S(1)} %bitcast.176, pred[1024,1024]{0,1:T(8,128)(4,1)S(1)} %broadcast_compare_fusion.4, f32[2,1024,128]{2,1,0:T(8,128)S(1)} %get-tuple-element.732, f32[2,1024]{1,0:T(2,128)S(1)} %get-tuple-element.716, ...), kind=kOutput, calls=%fused_computation.38.clone.1 | convolution fusion | flops 548143104 | bytes 11812873 | tf_op jit(solution)/shard_map/while/body/eval_jaxpr/pqk,kd->pqd/dot_general | solution.py:75
  185.3 6.0 %fusion.98 = (f32[2,1024]{1,0:T(2,128)S(1)}, f32[1024,1024,2]{1,0,2:T(8,128)}) fusion(pred[1024,1024]{0,1:T(8,128)(4,1)S(1)} %broadcast_compare_fusion.4, bf16[1024,2,128]{2,0,1:T(8,128)(2,1)S(1)} %get-tuple-element.746, bf16[2,8192,128]{2,1,0:T(8,128)(2,1)} %get-tuple-element.745, s32[]{:T(128)S(6)} %select_n.332), kind=kOutput, calls=%fused_computation.32.clone.1 | convolution fusion | flops 543160320 | bytes 10231812 | tf_op jit(solution)/shard_map/while/body/eval_jaxpr/qpd,kd->pqk/dot_general | solution.py:69
  191.3 4.6 %fusion.100 = f32[2,1024]{1,0:T(2,128)S(1)} fusion(f32[1024,1024,2]{1,0,2:T(8,128)} %get-tuple-element.715, f32[2,1024]{1,0:T(2,128)S(1)} %bitcast.175, pred[1024,1024]{0,1:T(8,128)(4,1)S(1)} %broadcast_compare_fusion.4), kind=kLoop, calls=%fused_computation.34.clone.1 | loop fusion | flops 10483712 | bytes 9453568 | tf_op jit(solution)/shard_map/while/body/eval_jaxpr/reduce_sum | solution.py:24
  195.9 5.3 %fusion.101 = f32[2,1024,128]{2,1,0:T(8,128)S(1)} fusion(f32[1024,1024,2]{1,0,2:T(8,128)} %get-tuple-element.715, f32[2,1024]{1,0:T(2,128)S(1)} %bitcast.176, pred[1024,1024]{0,1:T(8,128)(4,1)S(1)} %broadcast_compare_fusion.4, f32[2,1024,128]{2,1,0:T(8,128)S(1)} %get-tuple-element.732, f32[2,1024]{1,0:T(2,128)S(1)} %get-tuple-element.716, ...), kind=kOutput, calls=%fused_computation.38.clone.1 | convolution fusion | flops 548143104 | bytes 11812873 | tf_op jit(solution)/shard_map/while/body/eval_jaxpr/pqk,kd->pqd/dot_general | solution.py:75
  201.3 15.3 %all-to-all-done.2 = bf16[128,1,2,12,2,8,128]{6,5,4,3,2,1,0:T(8,128)(2,1)} async-done(((bf16[128,1,2,12,2,8,128]{6,5,4,3,2,1,0:T(8,128)(2,1)}), bf16[128,1,2,12,2,8,128]{6,5,4,3,2,1,0:T(8,128)(2,1)}, u32[]{:S(2)}, u32[]{:S(2)}) %all-to-all-start.2) | async-done | bytes 12582944 | tf_op jit(solution)/shard_map/all_to_all | solution.py:102
  216.6 11.6 %copy.64 = bf16[2,8,12,2,16,8,128]{6,5,4,3,2,1,0:T(8,128)(2,1)} copy(bf16[2,8,12,2,16,8,128]{6,5,3,2,0,1,4:T(8,128)(2,1)} %bitcast.20) | data formatting | bytes 25165824 | tf_op jit(solution)/shard_map/transpose | solution.py:104
  228.2 105.4 %while.40 = (s32[]{:T(128)}, f32[2,1024,1]{1,0,2:T(2,128)S(1)}, f32[2,1024,1]{1,0,2:T(2,128)S(1)}, f32[2,1024,128]{2,1,0:T(8,128)S(1)}, pred[8,2,12]{2,1,0:T(4,1...) while((s32[]{:T(128)}, f32[2,1024,1]{1,0,2:T(2,128)S(1)}, ...), condition=%wide.region_11.12_spmd, body=%wide.region_8.11_spmd.sunk | while | flops 1652037632 | bytes 45238536 | solution.py:128
  228.3 1.5 constant_dynamic-slice_fusion.4
  229.8 2.8 bitcast_reduce_fusion.2
  232.6 3.5 fusion.93
  236.2 5.2 %fusion.94 = f32[2,1024,128]{2,1,0:T(8,128)S(1)} fusion(bf16[2,1536,128]{2,1,0:T(8,128)(2,1)S(1)} %bitcast.168, f32[2,1536,1024]{2,1,0:T(8,128)S(1)} %get-tuple-element.701, f32[2,1024]{1,0:T(2,128)S(1)} %bitcast.174, pred[2,1536]{1,0:T(4,128)(4,1)S(1)} %bitcast.172, f32[2,1024,128]{2,1,0:T(8,128)S(1)} %get-tuple-element.768, ...), kind=kOutput, calls=%fused_computation.17.clone.1 | convolution fusion | flops 821559296 | bytes 15485952 | tf_op jit(solution)/shard_map/while/body/eval_jaxpr/pqk,pkd->pqd/dot_general | solution.py:122
  241.4 1.5 constant_dynamic-slice_fusion.4
  242.9 2.8 bitcast_reduce_fusion.2
  245.8 3.5 fusion.93
  249.3 5.2 %fusion.94 = f32[2,1024,128]{2,1,0:T(8,128)S(1)} fusion(bf16[2,1536,128]{2,1,0:T(8,128)(2,1)S(1)} %bitcast.168, f32[2,1536,1024]{2,1,0:T(8,128)S(1)} %get-tuple-element.701, f32[2,1024]{1,0:T(2,128)S(1)} %bitcast.174, pred[2,1536]{1,0:T(4,128)(4,1)S(1)} %bitcast.172, f32[2,1024,128]{2,1,0:T(8,128)S(1)} %get-tuple-element.768, ...), kind=kOutput, calls=%fused_computation.17.clone.1 | convolution fusion | flops 821559296 | bytes 15485952 | tf_op jit(solution)/shard_map/while/body/eval_jaxpr/pqk,pkd->pqd/dot_general | solution.py:122
  256.1 2.8 bitcast_reduce_fusion.2
  259.0 3.5 fusion.93
  262.5 5.2 %fusion.94 = f32[2,1024,128]{2,1,0:T(8,128)S(1)} fusion(bf16[2,1536,128]{2,1,0:T(8,128)(2,1)S(1)} %bitcast.168, f32[2,1536,1024]{2,1,0:T(8,128)S(1)} %get-tuple-element.701, f32[2,1024]{1,0:T(2,128)S(1)} %bitcast.174, pred[2,1536]{1,0:T(4,128)(4,1)S(1)} %bitcast.172, f32[2,1024,128]{2,1,0:T(8,128)S(1)} %get-tuple-element.768, ...), kind=kOutput, calls=%fused_computation.17.clone.1 | convolution fusion | flops 821559296 | bytes 15485952 | tf_op jit(solution)/shard_map/while/body/eval_jaxpr/pqk,pkd->pqd/dot_general | solution.py:122
  269.3 2.8 bitcast_reduce_fusion.2
  272.2 3.5 fusion.93
  275.7 5.2 %fusion.94 = f32[2,1024,128]{2,1,0:T(8,128)S(1)} fusion(bf16[2,1536,128]{2,1,0:T(8,128)(2,1)S(1)} %bitcast.168, f32[2,1536,1024]{2,1,0:T(8,128)S(1)} %get-tuple-element.701, f32[2,1024]{1,0:T(2,128)S(1)} %bitcast.174, pred[2,1536]{1,0:T(4,128)(4,1)S(1)} %bitcast.172, f32[2,1024,128]{2,1,0:T(8,128)S(1)} %get-tuple-element.768, ...), kind=kOutput, calls=%fused_computation.17.clone.1 | convolution fusion | flops 821559296 | bytes 15485952 | tf_op jit(solution)/shard_map/while/body/eval_jaxpr/pqk,pkd->pqd/dot_general | solution.py:122
  282.5 2.8 bitcast_reduce_fusion.2
  285.3 3.5 fusion.93
  288.9 5.2 %fusion.94 = f32[2,1024,128]{2,1,0:T(8,128)S(1)} fusion(bf16[2,1536,128]{2,1,0:T(8,128)(2,1)S(1)} %bitcast.168, f32[2,1536,1024]{2,1,0:T(8,128)S(1)} %get-tuple-element.701, f32[2,1024]{1,0:T(2,128)S(1)} %bitcast.174, pred[2,1536]{1,0:T(4,128)(4,1)S(1)} %bitcast.172, f32[2,1024,128]{2,1,0:T(8,128)S(1)} %get-tuple-element.768, ...), kind=kOutput, calls=%fused_computation.17.clone.1 | convolution fusion | flops 821559296 | bytes 15485952 | tf_op jit(solution)/shard_map/while/body/eval_jaxpr/pqk,pkd->pqd/dot_general | solution.py:122
  295.7 2.8 bitcast_reduce_fusion.2
  298.5 3.5 fusion.93
  302.1 5.2 %fusion.94 = f32[2,1024,128]{2,1,0:T(8,128)S(1)} fusion(bf16[2,1536,128]{2,1,0:T(8,128)(2,1)S(1)} %bitcast.168, f32[2,1536,1024]{2,1,0:T(8,128)S(1)} %get-tuple-element.701, f32[2,1024]{1,0:T(2,128)S(1)} %bitcast.174, pred[2,1536]{1,0:T(4,128)(4,1)S(1)} %bitcast.172, f32[2,1024,128]{2,1,0:T(8,128)S(1)} %get-tuple-element.768, ...), kind=kOutput, calls=%fused_computation.17.clone.1 | convolution fusion | flops 821559296 | bytes 15485952 | tf_op jit(solution)/shard_map/while/body/eval_jaxpr/pqk,pkd->pqd/dot_general | solution.py:122
  308.8 2.8 bitcast_reduce_fusion.2
  311.7 3.5 fusion.93
  315.2 5.2 %fusion.94 = f32[2,1024,128]{2,1,0:T(8,128)S(1)} fusion(bf16[2,1536,128]{2,1,0:T(8,128)(2,1)S(1)} %bitcast.168, f32[2,1536,1024]{2,1,0:T(8,128)S(1)} %get-tuple-element.701, f32[2,1024]{1,0:T(2,128)S(1)} %bitcast.174, pred[2,1536]{1,0:T(4,128)(4,1)S(1)} %bitcast.172, f32[2,1024,128]{2,1,0:T(8,128)S(1)} %get-tuple-element.768, ...), kind=kOutput, calls=%fused_computation.17.clone.1 | convolution fusion | flops 821559296 | bytes 15485952 | tf_op jit(solution)/shard_map/while/body/eval_jaxpr/pqk,pkd->pqd/dot_general | solution.py:122
  322.0 2.8 bitcast_reduce_fusion.2
  324.9 3.5 fusion.93
  328.4 5.2 %fusion.94 = f32[2,1024,128]{2,1,0:T(8,128)S(1)} fusion(bf16[2,1536,128]{2,1,0:T(8,128)(2,1)S(1)} %bitcast.168, f32[2,1536,1024]{2,1,0:T(8,128)S(1)} %get-tuple-element.701, f32[2,1024]{1,0:T(2,128)S(1)} %bitcast.174, pred[2,1536]{1,0:T(4,128)(4,1)S(1)} %bitcast.172, f32[2,1024,128]{2,1,0:T(8,128)S(1)} %get-tuple-element.768, ...), kind=kOutput, calls=%fused_computation.17.clone.1 | convolution fusion | flops 821559296 | bytes 15485952 | tf_op jit(solution)/shard_map/while/body/eval_jaxpr/pqk,pkd->pqd/dot_general | solution.py:122
  334.8 23.9 %all_to_all.55 = bf16[16,64,256]{2,1,0:T(8,128)(2,1)S(1)} all-to-all(bf16[16,64,256]{2,1,0:T(8,128)(2,1)S(1)} %reshape.344), channel_id=1, replica_groups=mesh['seq'=16,'ctx'=8] {'seq'}, dimensions={0} | all-to-all | bytes 1048576 | tf_op jit(solution)/shard_map/all_to_all | solution.py:132
  (142 shorter events, 22.8 us)
Async XLA Ops:
  6.5 1.0 copy-start
  6.5 26.9 %copy-start.2 = (s32[1024]{0:T(1024)S(1)}, s32[1024]{0:T(1024)}, u32[]{:S(2)}) copy-start(s32[1024]{0:T(1024)} %param.15) | copy-start | bytes 12292
  6.5 61.0 %all-gather.2.cloned.1.call-start = ((), (), s32[]{:S(2)}) async-start(), calls=%async_computation.4 | async-start | bytes 4718592 | tf_op jit(solution)/shard_map/all_gather | solution.py:63
  28.3 19.2 %all-to-all-start.1 = ((bf16[64,16,256]{2,0,1:T(8,128)(2,1)}), bf16[64,16,256]{2,0,1:T(8,128)(2,1)S(1)}, u32[]{:S(2)}, u32[]{:S(2)}) async-start(bf16[64,16,256]{2,0,1:T(8,128)(2,1)} %bitcast.118), calls=%async_computation.1 | async-start | bytes 1048576 | tf_op jit(solution)/shard_map/all_to_all | solution.py:49
  55.6 161.0 %all-to-all-start.2 = ((bf16[128,1,2,12,2,8,128]{6,5,4,3,2,1,0:T(8,128)(2,1)}), bf16[128,1,2,12,2,8,128]{6,5,4,3,2,1,0:T(8,128)(2,1)}, u32[]{:S(2)}, u32[]{:S(2)}) async-start(bf16[128,1,2,12,2,8,128]{6,5,4,3,2,1,0:T(8,128)(2,1)} %bitcast.166), calls=%async_computation.2 | async-start | bytes 25165824 | tf_op jit(solution)/shard_map/all_to_all | solution.py:102
  333.6 26.0 %copy-start.1 = (bf16[2,64,1024]{2,1,0:T(8,128)(2,1)S(1)}, bf16[2,64,1024]{2,1,0:T(8,128)(2,1)}, u32[]{:S(2)}) copy-start(bf16[2,64,1024]{2,1,0:T(8,128)(2,1)} %param.11) | copy-start | bytes 786436
Sparse Core Ops, SparseCore 0:
  26.6 30.3 all-gather.1
where the time goes:
time: 367 us; the launch traced here: 366 us
  matrix products  154 us (42%)
  other arithmetic  76.5 us (21%)
  local copies, waits for them, and re-layouts  48.3 us (13%)
  blocking collectives  41.8 us (11%)
  starting transfers between devices  15.3 us (4%)
  waiting for transfers between devices  15.3 us (4%)
  between operations  13.6 us (4%)
    reduce_sum x16, other arithmetic, online_update(): new_sum = running_sum * fading + jnp.sum(weights, axis=2, keepdims=True)  64.7 us
    dot_general x8, matrix products, visit(): jnp.einsum('qpd,kd->pqk', own_queries, shard_kv[0], preferred_element_typ...  47.7 us
    dot_general x8, matrix products, stretch_mix(): jnp.einsum('pqk,kd->pqd', rounded, shard_kv[1], preferred_element_type=jn...  42.8 us
    dot_general x8, matrix products, block_mix(): jnp.einsum('pqk,pkd->pqd', rounded, block_values, preferred_element_type=...  41.2 us
    all_to_all x1, blocking collectives, on_device(): lax.all_to_all(outgoing, 'seq', split_axis=0, concat_axis=2, tiled=True)  23.9 us
    dot_general x8, matrix products, visit(): jnp.einsum('qpd,pkd->pqk', own_queries, block_keys, preferred_element_typ...  22.7 us
    all_to_all x1, blocking collectives, on_device(): lax.all_to_all(widened_kv, 'seq', split_axis=2, concat_axis=1, tiled=True)  17.9 us
    all_to_all x1, waiting for transfers between devices, on_device(): lax.all_to_all(widened, ('seq', 'ctx'), split_axis=0, concat_axis=1, tile...  15.3 us
  transfers between devices with their start and end apart: 3, of which 1 were waited for; matrix products, arithmetic and copies ran while one was open for 43% of the time, Pallas kernels for 0%

commit v1 on v0

--- a/solution.py
+++ b/solution.py
@@ -9,6 +9,19 @@
 BLK = 128
 CAP = 12
 masked_value = -1e30
+
+
+def expand_pipes(x_local):
+    a_next = jnp.concatenate(
+        lax.all_to_all(
+            jnp.stack(jnp.split(x_local, lax.psum(1, axis_name="seq"), 2)),
+            axis_name="seq",
+            split_axis=0,
+            concat_axis=0,
+        ),
+        1,
+    )
+    return a_next
 
 
 def stretch_positions(rows, shard, tok_rows, n_ctx):
@@ -50,9 +63,7 @@
         sent_queries, "seq", split_axis=1, concat_axis=0, tiled=True
     ).reshape(query_rows, per_device, HD)
     widened_kv = jnp.repeat(stretch_kv.reshape(2, tok_rows, KVH, HD), n_seq // KVH, axis=2)
-    own_kv = lax.all_to_all(widened_kv, "seq", split_axis=2, concat_axis=1, tiled=True).reshape(
-        2, query_rows, HD
-    )
+    own_kv = expand_pipes(widened_kv).reshape(2, query_rows, HD)
     row_index = jnp.arange(query_rows, dtype=jnp.int32)
     query_position = stretch_positions(row_index, ctx_index, tok_rows, n_ctx)
     start_carry = (

time: 367 us -> 368 us (level)
  other arithmetic: 76.5 us -> 57.5 us
  waiting for transfers between devices: 15.3 us -> 29.8 us
    reduce_sum x16, other arithmetic: 64.7 us -> 45.7 us  [online_update(): new_sum = running_sum * fading + jnp.sum(weights, axis=2, keepdims=True)]
    all_to_all x1, waiting for transfers between devices: 15.3 us -> 29.7 us  [on_device(): lax.all_to_all(widened, ('seq', 'ctx'), split_axis=0, concat_axis=1, tile...]
  transfers between devices with their start and end apart: 3 -> 3, of which waited for: 1 -> 1; matrix products, arithmetic and copies ran while one was open for 43% -> 38% of each run, Pallas kernels for 0% -> 0%
where the time goes in v1:
time: 368 us; the launch traced here: 367 us
  matrix products  156 us (42%)
  other arithmetic  57.5 us (16%)
  local copies, waits for them, and re-layouts  51.7 us (14%)
  blocking collectives  42 us (11%)
  waiting for transfers between devices  29.8 us (8%)
  starting transfers between devices  15.3 us (4%)
  between operations  13.7 us (4%)
    dot_general x8, matrix products, visit(): jnp.einsum('qpd,kd->pqk', own_queries, shard_kv[0], preferred_element_typ...  47.7 us
    reduce_sum x16, other arithmetic, online_update(): new_sum = running_sum * fading + jnp.sum(weights, axis=2, keepdims=True)  45.7 us
    dot_general x8, matrix products, stretch_mix(): jnp.einsum('pqk,kd->pqd', rounded, shard_kv[1], preferred_element_type=jn...  44 us
    dot_general x8, matrix products, block_mix(): jnp.einsum('pqk,pkd->pqd', rounded, block_values, preferred_element_type=...  41.1 us
    all_to_all x1, waiting for transfers between devices, on_device(): lax.all_to_all(widened, ('seq', 'ctx'), split_axis=0, concat_axis=1, tile...  29.7 us
    all_to_all x1, blocking collectives, on_device(): lax.all_to_all(outgoing, 'seq', split_axis=0, concat_axis=2, tiled=True)  24.1 us
    dot_general x8, matrix products, visit(): jnp.einsum('qpd,pkd->pqk', own_queries, block_keys, preferred_element_typ...  22.7 us
    all_to_all x1, blocking collectives, expand_pipes(): lax.all_to_all(jnp.stack(jnp.split(x_local, lax.psum(1, axis_name='seq'),...  17.9 us
  transfers between devices with their start and end apart: 3, of which 1 were waited for; matrix products, arithmetic and copies ran while one was open for 38% of the time, Pallas kernels for 0%

profile of v1, /device:TPU:9, one launch (start us, length us, event | category | flops | bytes accessed | tf_op | source)
XLA Modules:
  0.0 366.7 jit_solution(12547652169963911107)
XLA Ops:
  7.9 17.9 %all_to_all.44 = bf16[16,2,64,1,128]{4,2,1,3,0:T(8,128)(2,1)S(1)} all-to-all(bf16[16,2,64,1,128]{4,2,1,3,0:T(8,128)(2,1)S(1)} %fusion.60), channel_id=1, replica_groups=mesh['seq'=16,'ctx'=8] {'seq'}, dimensions={0} | all-to-all | bytes 1048576 | tf_op jit(solution)/shard_map/all_to_all | solution.py:16
  26.7 1.9 copy.129
  28.6 3.6 all-to-all-start.1
  33.7 4.5 %gather_fusion = s32[1024]{0:T(1024)S(1)} fusion(s32[1024]{0:T(1024)S(1)} %copy-done.2, s32[1024]{0:T(1024)S(1)} %broadcast_clamp_fusion), kind=kCustom, calls=%fused_computation | custom fusion | bytes 12288 | tf_op jit(solution)/shard_map/gather | solution.py:97
  38.4 1.5 reduce_window_sum.22
  40.1 1.7 fusion.57
  42.7 5.2 %gather_fusion.1 = bf16[384,2,8,128]{3,2,1,0:T(8,128)(2,1)S(1)} fusion(bf16[128,2,8,8,128]{4,3,2,1,0:T(8,128)(2,1)} %param.12, s32[384]{0:T(512)S(1)} %reshape.353), kind=kCustom, calls=%fused_computation.1 | custom fusion | bytes 3148800 | tf_op jit(solution)/shard_map/gather | solution.py:108
  47.8 8.0 %broadcast_in_dim.202 = bf16[16,8,2,12,2,8,128]{6,5,4,3,2,1,0:T(8,128)(2,1)} broadcast(bf16[16,2,12,2,8,128]{5,4,3,2,1,0:T(8,128)(2,1)S(1)} %bitcast.231), dimensions={0,2,3,4,5,6} | broadcast | bytes 14155776 | tf_op jit(solution)/shard_map/broadcast_in_dim | solution.py:110
  55.8 11.8 %all-to-all-start.2 = ((bf16[128,1,2,12,2,8,128]{6,5,4,3,2,1,0:T(8,128)(2,1)}), bf16[128,1,2,12,2,8,128]{6,5,4,3,2,1,0:T(8,128)(2,1)}, u32[]{:S(2)}, u32[]{:S(2)}) async-start(bf16[128,1,2,12,2,8,128]{6,5,4,3,2,1,0:T(8,128)(2,1)} %bitcast.228), calls=%async_computation.2 | async-start | bytes 25165824 | tf_op jit(solution)/shard_map/all_to_all | solution.py:113
  67.8 119.3 %while.41 = (s32[]{:T(128)}, f32[2,1024,1]{1,0,2:T(2,128)S(1)}, f32[2,1024,1]{1,0,2:T(2,128)S(1)}, f32[2,1024,128]{2,1,0:T(8,128)S(1)}, bf16[2,8192,128]{2,1,0:T...) while((s32[]{:T(128)}, f32[2,1024,1]{1,0,2:T(2,128)S(1)}, ...), condition=%wide.region_3.4_spmd.clone.clone, body=%wide.region_0.3_spmd.clone.clone.sunk | while | flops 1102876672 | bytes 66210024 | solution.py:92
  68.5 6.0 %fusion.114 = (f32[2,1024]{1,0:T(2,128)S(1)}, f32[1024,1024,2]{1,0,2:T(8,128)}) fusion(pred[1024,1024]{0,1:T(8,128)(4,1)S(1)} %broadcast_compare_fusion.4, bf16[1024,2,128]{2,0,1:T(8,128)(2,1)S(1)} %get-tuple-element.746, bf16[2,8192,128]{2,1,0:T(8,128)(2,1)} %get-tuple-element.745, s32[]{:T(128)S(6)} %select_n.332), kind=kOutput, calls=%fused_computation.32.clone.1 | convolution fusion | flops 543160320 | bytes 10231812 | tf_op jit(solution)/shard_map/while/body/eval_jaxpr/qpd,kd->pqk/dot_general | solution.py:80
  74.5 5.5 %fusion.117 = f32[2,1024,128]{2,1,0:T(8,128)S(1)} fusion(f32[1024,1024,2]{1,0,2:T(8,128)} %get-tuple-element.715, f32[2,1024]{1,0:T(2,128)S(1)} %bitcast.237, pred[1024,1024]{0,1:T(8,128)(4,1)S(1)} %broadcast_compare_fusion.4, f32[2,1024,128]{2,1,0:T(8,128)S(1)} %get-tuple-element.732, f32[2,1024]{1,0:T(2,128)S(1)} %get-tuple-element.716, ...), kind=kOutput, calls=%fused_computation.38.clone.1 | convolution fusion | flops 548143104 | bytes 11812873 | tf_op jit(solution)/shard_map/while/body/eval_jaxpr/pqk,kd->pqd/dot_general | solution.py:86
  80.4 2.2 fusion.116
  83.4 6.0 %fusion.114 = (f32[2,1024]{1,0:T(2,128)S(1)}, f32[1024,1024,2]{1,0,2:T(8,128)}) fusion(pred[1024,1024]{0,1:T(8,128)(4,1)S(1)} %broadcast_compare_fusion.4, bf16[1024,2,128]{2,0,1:T(8,128)(2,1)S(1)} %get-tuple-element.746, bf16[2,8192,128]{2,1,0:T(8,128)(2,1)} %get-tuple-element.745, s32[]{:T(128)S(6)} %select_n.332), kind=kOutput, calls=%fused_computation.32.clone.1 | convolution fusion | flops 543160320 | bytes 10231812 | tf_op jit(solution)/shard_map/while/body/eval_jaxpr/qpd,kd->pqk/dot_general | solution.py:80
  89.4 5.5 %fusion.117 = f32[2,1024,128]{2,1,0:T(8,128)S(1)} fusion(f32[1024,1024,2]{1,0,2:T(8,128)} %get-tuple-element.715, f32[2,1024]{1,0:T(2,128)S(1)} %bitcast.237, pred[1024,1024]{0,1:T(8,128)(4,1)S(1)} %broadcast_compare_fusion.4, f32[2,1024,128]{2,1,0:T(8,128)S(1)} %get-tuple-element.732, f32[2,1024]{1,0:T(2,128)S(1)} %get-tuple-element.716, ...), kind=kOutput, calls=%fused_computation.38.clone.1 | convolution fusion | flops 548143104 | bytes 11812873 | tf_op jit(solution)/shard_map/while/body/eval_jaxpr/pqk,kd->pqd/dot_general | solution.py:86
  95.3 2.2 fusion.116
  98.4 6.0 %fusion.114 = (f32[2,1024]{1,0:T(2,128)S(1)}, f32[1024,1024,2]{1,0,2:T(8,128)}) fusion(pred[1024,1024]{0,1:T(8,128)(4,1)S(1)} %broadcast_compare_fusion.4, bf16[1024,2,128]{2,0,1:T(8,128)(2,1)S(1)} %get-tuple-element.746, bf16[2,8192,128]{2,1,0:T(8,128)(2,1)} %get-tuple-element.745, s32[]{:T(128)S(6)} %select_n.332), kind=kOutput, calls=%fused_computation.32.clone.1 | convolution fusion | flops 543160320 | bytes 10231812 | tf_op jit(solution)/shard_map/while/body/eval_jaxpr/qpd,kd->pqk/dot_general | solution.py:80
  104.3 5.5 %fusion.117 = f32[2,1024,128]{2,1,0:T(8,128)S(1)} fusion(f32[1024,1024,2]{1,0,2:T(8,128)} %get-tuple-element.715, f32[2,1024]{1,0:T(2,128)S(1)} %bitcast.237, pred[1024,1024]{0,1:T(8,128)(4,1)S(1)} %broadcast_compare_fusion.4, f32[2,1024,128]{2,1,0:T(8,128)S(1)} %get-tuple-element.732, f32[2,1024]{1,0:T(2,128)S(1)} %get-tuple-element.716, ...), kind=kOutput, calls=%fused_computation.38.clone.1 | convolution fusion | flops 548143104 | bytes 11812873 | tf_op jit(solution)/shard_map/while/body/eval_jaxpr/pqk,kd->pqd/dot_general | solution.py:86
  110.3 2.2 fusion.116
  113.3 6.0 %fusion.114 = (f32[2,1024]{1,0:T(2,128)S(1)}, f32[1024,1024,2]{1,0,2:T(8,128)}) fusion(pred[1024,1024]{0,1:T(8,128)(4,1)S(1)} %broadcast_compare_fusion.4, bf16[1024,2,128]{2,0,1:T(8,128)(2,1)S(1)} %get-tuple-element.746, bf16[2,8192,128]{2,1,0:T(8,128)(2,1)} %get-tuple-element.745, s32[]{:T(128)S(6)} %select_n.332), kind=kOutput, calls=%fused_computation.32.clone.1 | convolution fusion | flops 543160320 | bytes 10231812 | tf_op jit(solution)/shard_map/while/body/eval_jaxpr/qpd,kd->pqk/dot_general | solution.py:80
  119.3 5.5 %fusion.117 = f32[2,1024,128]{2,1,0:T(8,128)S(1)} fusion(f32[1024,1024,2]{1,0,2:T(8,128)} %get-tuple-element.715, f32[2,1024]{1,0:T(2,128)S(1)} %bitcast.237, pred[1024,1024]{0,1:T(8,128)(4,1)S(1)} %broadcast_compare_fusion.4, f32[2,1024,128]{2,1,0:T(8,128)S(1)} %get-tuple-element.732, f32[2,1024]{1,0:T(2,128)S(1)} %get-tuple-element.716, ...), kind=kOutput, calls=%fused_computation.38.clone.1 | convolution fusion | flops 548143104 | bytes 11812873 | tf_op jit(solution)/shard_map/while/body/eval_jaxpr/pqk,kd->pqd/dot_general | solution.py:86
  125.2 2.2 fusion.116
  128.2 6.0 %fusion.114 = (f32[2,1024]{1,0:T(2,128)S(1)}, f32[1024,1024,2]{1,0,2:T(8,128)}) fusion(pred[1024,1024]{0,1:T(8,128)(4,1)S(1)} %broadcast_compare_fusion.4, bf16[1024,2,128]{2,0,1:T(8,128)(2,1)S(1)} %get-tuple-element.746, bf16[2,8192,128]{2,1,0:T(8,128)(2,1)} %get-tuple-element.745, s32[]{:T(128)S(6)} %select_n.332), kind=kOutput, calls=%fused_computation.32.clone.1 | convolution fusion | flops 543160320 | bytes 10231812 | tf_op jit(solution)/shard_map/while/body/eval_jaxpr/qpd,kd->pqk/dot_general | solution.py:80
  134.2 5.5 %fusion.117 = f32[2,1024,128]{2,1,0:T(8,128)S(1)} fusion(f32[1024,1024,2]{1,0,2:T(8,128)} %get-tuple-element.715, f32[2,1024]{1,0:T(2,128)S(1)} %bitcast.237, pred[1024,1024]{0,1:T(8,128)(4,1)S(1)} %broadcast_compare_fusion.4, f32[2,1024,128]{2,1,0:T(8,128)S(1)} %get-tuple-element.732, f32[2,1024]{1,0:T(2,128)S(1)} %get-tuple-element.716, ...), kind=kOutput, calls=%fused_computation.38.clone.1 | convolution fusion | flops 548143104 | bytes 11812873 | tf_op jit(solution)/shard_map/while/body/eval_jaxpr/pqk,kd->pqd/dot_general | solution.py:86
  140.1 2.2 fusion.116
  143.1 6.0 %fusion.114 = (f32[2,1024]{1,0:T(2,128)S(1)}, f32[1024,1024,2]{1,0,2:T(8,128)}) fusion(pred[1024,1024]{0,1:T(8,128)(4,1)S(1)} %broadcast_compare_fusion.4, bf16[1024,2,128]{2,0,1:T(8,128)(2,1)S(1)} %get-tuple-element.746, bf16[2,8192,128]{2,1,0:T(8,128)(2,1)} %get-tuple-element.745, s32[]{:T(128)S(6)} %select_n.332), kind=kOutput, calls=%fused_computation.32.clone.1 | convolution fusion | flops 543160320 | bytes 10231812 | tf_op jit(solution)/shard_map/while/body/eval_jaxpr/qpd,kd->pqk/dot_general | solution.py:80
  149.1 5.5 %fusion.117 = f32[2,1024,128]{2,1,0:T(8,128)S(1)} fusion(f32[1024,1024,2]{1,0,2:T(8,128)} %get-tuple-element.715, f32[2,1024]{1,0:T(2,128)S(1)} %bitcast.237, pred[1024,1024]{0,1:T(8,128)(4,1)S(1)} %broadcast_compare_fusion.4, f32[2,1024,128]{2,1,0:T(8,128)S(1)} %get-tuple-element.732, f32[2,1024]{1,0:T(2,128)S(1)} %get-tuple-element.716, ...), kind=kOutput, calls=%fused_computation.38.clone.1 | convolution fusion | flops 548143104 | bytes 11812873 | tf_op jit(solution)/shard_map/while/body/eval_jaxpr/pqk,kd->pqd/dot_general | solution.py:86
  155.0 2.2 fusion.116
  158.0 6.0 %fusion.114 = (f32[2,1024]{1,0:T(2,128)S(1)}, f32[1024,1024,2]{1,0,2:T(8,128)}) fusion(pred[1024,1024]{0,1:T(8,128)(4,1)S(1)} %broadcast_compare_fusion.4, bf16[1024,2,128]{2,0,1:T(8,128)(2,1)S(1)} %get-tuple-element.746, bf16[2,8192,128]{2,1,0:T(8,128)(2,1)} %get-tuple-element.745, s32[]{:T(128)S(6)} %select_n.332), kind=kOutput, calls=%fused_computation.32.clone.1 | convolution fusion | flops 543160320 | bytes 10231812 | tf_op jit(solution)/shard_map/while/body/eval_jaxpr/qpd,kd->pqk/dot_general | solution.py:80
  164.0 5.5 %fusion.117 = f32[2,1024,128]{2,1,0:T(8,128)S(1)} fusion(f32[1024,1024,2]{1,0,2:T(8,128)} %get-tuple-element.715, f32[2,1024]{1,0:T(2,128)S(1)} %bitcast.237, pred[1024,1024]{0,1:T(8,128)(4,1)S(1)} %broadcast_compare_fusion.4, f32[2,1024,128]{2,1,0:T(8,128)S(1)} %get-tuple-element.732, f32[2,1024]{1,0:T(2,128)S(1)} %get-tuple-element.716, ...), kind=kOutput, calls=%fused_computation.38.clone.1 | convolution fusion | flops 548143104 | bytes 11812873 | tf_op jit(solution)/shard_map/while/body/eval_jaxpr/pqk,kd->pqd/dot_general | solution.py:86
  169.9 2.2 fusion.116
  172.9 6.0 %fusion.114 = (f32[2,1024]{1,0:T(2,128)S(1)}, f32[1024,1024,2]{1,0,2:T(8,128)}) fusion(pred[1024,1024]{0,1:T(8,128)(4,1)S(1)} %broadcast_compare_fusion.4, bf16[1024,2,128]{2,0,1:T(8,128)(2,1)S(1)} %get-tuple-element.746, bf16[2,8192,128]{2,1,0:T(8,128)(2,1)} %get-tuple-element.745, s32[]{:T(128)S(6)} %select_n.332), kind=kOutput, calls=%fused_computation.32.clone.1 | convolution fusion | flops 543160320 | bytes 10231812 | tf_op jit(solution)/shard_map/while/body/eval_jaxpr/qpd,kd->pqk/dot_general | solution.py:80
  178.9 5.5 %fusion.117 = f32[2,1024,128]{2,1,0:T(8,128)S(1)} fusion(f32[1024,1024,2]{1,0,2:T(8,128)} %get-tuple-element.715, f32[2,1024]{1,0:T(2,128)S(1)} %bitcast.237, pred[1024,1024]{0,1:T(8,128)(4,1)S(1)} %broadcast_compare_fusion.4, f32[2,1024,128]{2,1,0:T(8,128)S(1)} %get-tuple-element.732, f32[2,1024]{1,0:T(2,128)S(1)} %get-tuple-element.716, ...), kind=kOutput, calls=%fused_computation.38.clone.1 | convolution fusion | flops 548143104 | bytes 11812873 | tf_op jit(solution)/shard_map/while/body/eval_jaxpr/pqk,kd->pqd/dot_general | solution.py:86
  184.8 2.2 fusion.116
  187.1 29.7 %all-to-all-done.2 = bf16[128,1,2,12,2,8,128]{6,5,4,3,2,1,0:T(8,128)(2,1)} async-done(((bf16[128,1,2,12,2,8,128]{6,5,4,3,2,1,0:T(8,128)(2,1)}), bf16[128,1,2,12,2,8,128]{6,5,4,3,2,1,0:T(8,128)(2,1)}, u32[]{:S(2)}, u32[]{:S(2)}) %all-to-all-start.2) | async-done | bytes 12582944 | tf_op jit(solution)/shard_map/all_to_all | solution.py:113
  216.8 11.6 %copy.109 = bf16[2,8,12,2,16,8,128]{6,5,4,3,2,1,0:T(8,128)(2,1)} copy(bf16[2,8,12,2,16,8,128]{6,5,3,2,0,1,4:T(8,128)(2,1)} %bitcast.35) | data formatting | bytes 25165824 | tf_op jit(solution)/shard_map/transpose | solution.py:115
  228.4 105.3 %while.40 = (s32[]{:T(128)}, f32[2,1024,1]{1,0,2:T(2,128)S(1)}, f32[2,1024,1]{1,0,2:T(2,128)S(1)}, f32[2,1024,128]{2,1,0:T(8,128)S(1)}, pred[8,2,12]{2,1,0:T(4,1...) while((s32[]{:T(128)}, f32[2,1024,1]{1,0,2:T(2,128)S(1)}, ...), condition=%wide.region_11.12_spmd, body=%wide.region_8.11_spmd.sunk | while | flops 1652037632 | bytes 45238528 | solution.py:139
  230.0 2.9 bitcast_reduce_fusion.2
  232.9 5.1 %fusion.110 = f32[2,1024,128]{2,1,0:T(8,128)S(1)} fusion(bf16[2,1536,128]{2,1,0:T(8,128)(2,1)S(1)} %bitcast.230, f32[2,1536,1024]{2,1,0:T(8,128)S(1)} %get-tuple-element.701, f32[2,1024]{1,0:T(2,128)S(1)} %bitcast.235, pred[2,1536]{1,0:T(4,128)(4,1)S(1)} %bitcast.233, f32[2,1024,128]{2,1,0:T(8,128)S(1)} %get-tuple-element.768, ...), kind=kOutput, calls=%fused_computation.17.clone.1 | convolution fusion | flops 821559296 | bytes 15485952 | tf_op jit(solution)/shard_map/while/body/eval_jaxpr/pqk,pkd->pqd/dot_general | solution.py:133
  238.0 3.5 fusion.109
  241.6 1.5 constant_dynamic-slice_fusion.4
  243.2 2.8 bitcast_reduce_fusion.2
  246.0 5.1 %fusion.110 = f32[2,1024,128]{2,1,0:T(8,128)S(1)} fusion(bf16[2,1536,128]{2,1,0:T(8,128)(2,1)S(1)} %bitcast.230, f32[2,1536,1024]{2,1,0:T(8,128)S(1)} %get-tuple-element.701, f32[2,1024]{1,0:T(2,128)S(1)} %bitcast.235, pred[2,1536]{1,0:T(4,128)(4,1)S(1)} %bitcast.233, f32[2,1024,128]{2,1,0:T(8,128)S(1)} %get-tuple-element.768, ...), kind=kOutput, calls=%fused_computation.17.clone.1 | convolution fusion | flops 821559296 | bytes 15485952 | tf_op jit(solution)/shard_map/while/body/eval_jaxpr/pqk,pkd->pqd/dot_general | solution.py:133
  251.2 3.5 fusion.109
  254.7 1.5 constant_dynamic-slice_fusion.4
  256.3 2.9 bitcast_reduce_fusion.2
  259.2 5.1 %fusion.110 = f32[2,1024,128]{2,1,0:T(8,128)S(1)} fusion(bf16[2,1536,128]{2,1,0:T(8,128)(2,1)S(1)} %bitcast.230, f32[2,1536,1024]{2,1,0:T(8,128)S(1)} %get-tuple-element.701, f32[2,1024]{1,0:T(2,128)S(1)} %bitcast.235, pred[2,1536]{1,0:T(4,128)(4,1)S(1)} %bitcast.233, f32[2,1024,128]{2,1,0:T(8,128)S(1)} %get-tuple-element.768, ...), kind=kOutput, calls=%fused_computation.17.clone.1 | convolution fusion | flops 821559296 | bytes 15485952 | tf_op jit(solution)/shard_map/while/body/eval_jaxpr/pqk,pkd->pqd/dot_general | solution.py:133
  264.4 3.5 fusion.109
  269.5 2.8 bitcast_reduce_fusion.2
  272.4 5.1 %fusion.110 = f32[2,1024,128]{2,1,0:T(8,128)S(1)} fusion(bf16[2,1536,128]{2,1,0:T(8,128)(2,1)S(1)} %bitcast.230, f32[2,1536,1024]{2,1,0:T(8,128)S(1)} %get-tuple-element.701, f32[2,1024]{1,0:T(2,128)S(1)} %bitcast.235, pred[2,1536]{1,0:T(4,128)(4,1)S(1)} %bitcast.233, f32[2,1024,128]{2,1,0:T(8,128)S(1)} %get-tuple-element.768, ...), kind=kOutput, calls=%fused_computation.17.clone.1 | convolution fusion | flops 821559296 | bytes 15485952 | tf_op jit(solution)/shard_map/while/body/eval_jaxpr/pqk,pkd->pqd/dot_general | solution.py:133
  277.5 3.5 fusion.109
  282.7 2.9 bitcast_reduce_fusion.2
  285.5 5.1 %fusion.110 = f32[2,1024,128]{2,1,0:T(8,128)S(1)} fusion(bf16[2,1536,128]{2,1,0:T(8,128)(2,1)S(1)} %bitcast.230, f32[2,1536,1024]{2,1,0:T(8,128)S(1)} %get-tuple-element.701, f32[2,1024]{1,0:T(2,128)S(1)} %bitcast.235, pred[2,1536]{1,0:T(4,128)(4,1)S(1)} %bitcast.233, f32[2,1024,128]{2,1,0:T(8,128)S(1)} %get-tuple-element.768, ...), kind=kOutput, calls=%fused_computation.17.clone.1 | convolution fusion | flops 821559296 | bytes 15485952 | tf_op jit(solution)/shard_map/while/body/eval_jaxpr/pqk,pkd->pqd/dot_general | solution.py:133
  290.7 3.5 fusion.109
  295.8 2.8 bitcast_reduce_fusion.2
  298.7 5.1 %fusion.110 = f32[2,1024,128]{2,1,0:T(8,128)S(1)} fusion(bf16[2,1536,128]{2,1,0:T(8,128)(2,1)S(1)} %bitcast.230, f32[2,1536,1024]{2,1,0:T(8,128)S(1)} %get-tuple-element.701, f32[2,1024]{1,0:T(2,128)S(1)} %bitcast.235, pred[2,1536]{1,0:T(4,128)(4,1)S(1)} %bitcast.233, f32[2,1024,128]{2,1,0:T(8,128)S(1)} %get-tuple-element.768, ...), kind=kOutput, calls=%fused_computation.17.clone.1 | convolution fusion | flops 821559296 | bytes 15485952 | tf_op jit(solution)/shard_map/while/body/eval_jaxpr/pqk,pkd->pqd/dot_general | solution.py:133
  303.9 3.5 fusion.109
  309.0 2.9 bitcast_reduce_fusion.2
  311.9 5.1 %fusion.110 = f32[2,1024,128]{2,1,0:T(8,128)S(1)} fusion(bf16[2,1536,128]{2,1,0:T(8,128)(2,1)S(1)} %bitcast.230, f32[2,1536,1024]{2,1,0:T(8,128)S(1)} %get-tuple-element.701, f32[2,1024]{1,0:T(2,128)S(1)} %bitcast.235, pred[2,1536]{1,0:T(4,128)(4,1)S(1)} %bitcast.233, f32[2,1024,128]{2,1,0:T(8,128)S(1)} %get-tuple-element.768, ...), kind=kOutput, calls=%fused_computation.17.clone.1 | convolution fusion | flops 821559296 | bytes 15485952 | tf_op jit(solution)/shard_map/while/body/eval_jaxpr/pqk,pkd->pqd/dot_general | solution.py:133
  317.0 3.5 fusion.109
  322.2 2.8 bitcast_reduce_fusion.2
  325.0 5.1 %fusion.110 = f32[2,1024,128]{2,1,0:T(8,128)S(1)} fusion(bf16[2,1536,128]{2,1,0:T(8,128)(2,1)S(1)} %bitcast.230, f32[2,1536,1024]{2,1,0:T(8,128)S(1)} %get-tuple-element.701, f32[2,1024]{1,0:T(2,128)S(1)} %bitcast.235, pred[2,1536]{1,0:T(4,128)(4,1)S(1)} %bitcast.233, f32[2,1024,128]{2,1,0:T(8,128)S(1)} %get-tuple-element.768, ...), kind=kOutput, calls=%fused_computation.17.clone.1 | convolution fusion | flops 821559296 | bytes 15485952 | tf_op jit(solution)/shard_map/while/body/eval_jaxpr/pqk,pkd->pqd/dot_general | solution.py:133
  330.2 3.5 fusion.109
  335.0 24.1 %all_to_all.45 = bf16[16,64,256]{2,1,0:T(8,128)(2,1)S(1)} all-to-all(bf16[16,64,256]{2,1,0:T(8,128)(2,1)S(1)} %reshape.343), channel_id=1, replica_groups=mesh['seq'=16,'ctx'=8] {'seq'}, dimensions={0} | all-to-all | bytes 1048576 | tf_op jit(solution)/shard_map/all_to_all | solution.py:143
  (174 shorter events, 26.2 us)
Async XLA Ops:
  6.5 1.0 copy-start
  6.5 27.2 %copy-start.2 = (s32[1024]{0:T(1024)S(1)}, s32[1024]{0:T(1024)}, u32[]{:S(2)}) copy-start(s32[1024]{0:T(1024)} %param.15) | copy-start | bytes 12292
  6.5 61.3 %all-gather.2.cloned.1.call-start = ((), (), s32[]{:S(2)}) async-start(), calls=%async_computation.4 | async-start | bytes 4718592 | tf_op jit(solution)/shard_map/all_gather | solution.py:74
  28.6 19.2 %all-to-all-start.1 = ((bf16[64,16,256]{2,0,1:T(8,128)(2,1)}), bf16[64,16,256]{2,0,1:T(8,128)(2,1)S(1)}, u32[]{:S(2)}, u32[]{:S(2)}) async-start(bf16[64,16,256]{2,0,1:T(8,128)(2,1)} %bitcast.180), calls=%async_computation.1 | async-start | bytes 1048576 | tf_op jit(solution)/shard_map/all_to_all | solution.py:62
  55.8 161.0 %all-to-all-start.2 = ((bf16[128,1,2,12,2,8,128]{6,5,4,3,2,1,0:T(8,128)(2,1)}), bf16[128,1,2,12,2,8,128]{6,5,4,3,2,1,0:T(8,128)(2,1)}, u32[]{:S(2)}, u32[]{:S(2)}) async-start(bf16[128,1,2,12,2,8,128]{6,5,4,3,2,1,0:T(8,128)(2,1)} %bitcast.228), calls=%async_computation.2 | async-start | bytes 25165824 | tf_op jit(solution)/shard_map/all_to_all | solution.py:113
  74.5 5.9 %copy-start.3 = (f32[1024,1024,2]{1,0,2:T(8,128)S(1)}, f32[1024,1024,2]{1,0,2:T(8,128)}, u32[]{:S(2)}) copy-start(f32[1024,1024,2]{1,0,2:T(8,128)} %get-tuple-element.715) | copy-start | bytes 25165828 | tf_op jit(solution)/shard_map/while
  89.4 5.9 %copy-start.3 = (f32[1024,1024,2]{1,0,2:T(8,128)S(1)}, f32[1024,1024,2]{1,0,2:T(8,128)}, u32[]{:S(2)}) copy-start(f32[1024,1024,2]{1,0,2:T(8,128)} %get-tuple-element.715) | copy-start | bytes 25165828 | tf_op jit(solution)/shard_map/while
  104.3 5.9 %copy-start.3 = (f32[1024,1024,2]{1,0,2:T(8,128)S(1)}, f32[1024,1024,2]{1,0,2:T(8,128)}, u32[]{:S(2)}) copy-start(f32[1024,1024,2]{1,0,2:T(8,128)} %get-tuple-element.715) | copy-start | bytes 25165828 | tf_op jit(solution)/shard_map/while
  119.2 5.9 %copy-start.3 = (f32[1024,1024,2]{1,0,2:T(8,128)S(1)}, f32[1024,1024,2]{1,0,2:T(8,128)}, u32[]{:S(2)}) copy-start(f32[1024,1024,2]{1,0,2:T(8,128)} %get-tuple-element.715) | copy-start | bytes 25165828 | tf_op jit(solution)/shard_map/while
  134.2 5.9 %copy-start.3 = (f32[1024,1024,2]{1,0,2:T(8,128)S(1)}, f32[1024,1024,2]{1,0,2:T(8,128)}, u32[]{:S(2)}) copy-start(f32[1024,1024,2]{1,0,2:T(8,128)} %get-tuple-element.715) | copy-start | bytes 25165828 | tf_op jit(solution)/shard_map/while
  149.1 5.9 %copy-start.3 = (f32[1024,1024,2]{1,0,2:T(8,128)S(1)}, f32[1024,1024,2]{1,0,2:T(8,128)}, u32[]{:S(2)}) copy-start(f32[1024,1024,2]{1,0,2:T(8,128)} %get-tuple-element.715) | copy-start | bytes 25165828 | tf_op jit(solution)/shard_map/while
  164.0 5.9 %copy-start.3 = (f32[1024,1024,2]{1,0,2:T(8,128)S(1)}, f32[1024,1024,2]{1,0,2:T(8,128)}, u32[]{:S(2)}) copy-start(f32[1024,1024,2]{1,0,2:T(8,128)} %get-tuple-element.715) | copy-start | bytes 25165828 | tf_op jit(solution)/shard_map/while
  178.9 5.9 %copy-start.3 = (f32[1024,1024,2]{1,0,2:T(8,128)S(1)}, f32[1024,1024,2]{1,0,2:T(8,128)}, u32[]{:S(2)}) copy-start(f32[1024,1024,2]{1,0,2:T(8,128)} %get-tuple-element.715) | copy-start | bytes 25165828 | tf_op jit(solution)/shard_map/while
  333.7 26.2 %copy-start.1 = (bf16[2,64,1024]{2,1,0:T(8,128)(2,1)S(1)}, bf16[2,64,1024]{2,1,0:T(8,128)(2,1)}, u32[]{:S(2)}) copy-start(bf16[2,64,1024]{2,1,0:T(8,128)(2,1)} %param.11) | copy-start | bytes 786436
Sparse Core Ops, SparseCore 0:
  26.8 30.3 all-gather.1
